TPU v7x, 128 devices: a whole 4x4x4 slice. The times are simulated.
128 devices in a mesh: orbit: 32 (over y, z, core), region: 4 (over x).
Axes of the slice: x: 4, y: 4, z: 4, core: 2. Of those that a mesh axis runs over, the one named last changes fastest.
Arguments:
- footprints: bfloat16 [40960, 64, 256], P(('orbit', 'region')), may hold values from -0.0625 to 0.0625
- block_sounding: int32 [40960], P(('orbit', 'region')), may hold values from 0 to 31
- block_tile: int32 [40960], P(('orbit', 'region')), may hold values from 0 to 31
- block_count: int32 [128], P(('orbit', 'region')), may hold values from 80 to 320, as said below
- observations: float32 [1024, 64, 128], P('orbit'), may hold values from -6 to 6
- obs_weight: float32 [1024, 64], P('orbit'), may hold values from 0.25 to 4
- prior_std: float32 [4, 32, 256], P('region', 'orbit'), may hold values from 0.4 to 4.8
Outputs:
- flux: float32 [4, 32, 256, 128], P('region', 'orbit')
- residual: float32 [4, 32, 256, 128], P('region', 'orbit')
Inputs may be any that keep to these rules, and one draw needn't show every extreme that they name: `block_sounding`: index of a sounding block among the 32 of the block's orbit index. `block_tile`: index of a tile among the 32 of the block's region; some tiles are named far more often than others. `block_count`: slots from this count on are unused; some device has all 320 slots live.
All inputs are finite; a program needn't handle non-finite values.
Results may differ from a plain program's by a relative error of at most 0.0068.
Values may be sent and summed in bfloat16 or wider, within the bound.
A program may use at most 128 MiB of HBM per device.

v0:
```python
import jax
import jax.numpy as jnp
from jax import lax
from jax.sharding import PartitionSpec as P

ITERS = 2
GROUP = 64


def local_forward(footprints, block_sounding, block_tile, live_count, whole, sb_count):
    rounds = (live_count + GROUP - 1) // GROUP
    positions = jnp.arange(GROUP, dtype=jnp.int32)
    width = whole.shape[2]

    def turn(turn_index, running):
        offset = turn_index * GROUP
        blocks_now = lax.dynamic_slice_in_dim(footprints, offset, GROUP, 0)
        sound_ids = lax.dynamic_slice_in_dim(block_sounding, offset, GROUP, 0)
        tile_ids = lax.dynamic_slice_in_dim(block_tile, offset, GROUP, 0)
        alive = offset + positions < live_count
        targets = jnp.where(alive, sound_ids, sb_count)
        products = jnp.einsum(
            "bsc,bcr->bsr", blocks_now, whole[tile_ids], preferred_element_type=jnp.float32
        )
        return running + jax.ops.segment_sum(products, targets, num_segments=sb_count)

    start_sum = jnp.zeros((sb_count, footprints.shape[1], width), jnp.float32)
    return lax.fori_loop(0, rounds, turn, start_sum)


def local_transpose(footprints, block_sounding, block_tile, live_count, weighted, tile_count):
    rounds = (live_count + GROUP - 1) // GROUP
    positions = jnp.arange(GROUP, dtype=jnp.int32)
    width = weighted.shape[2]

    def turn(turn_index, running):
        offset = turn_index * GROUP
        blocks_now = lax.dynamic_slice_in_dim(footprints, offset, GROUP, 0)
        sound_ids = lax.dynamic_slice_in_dim(block_sounding, offset, GROUP, 0)
        tile_ids = lax.dynamic_slice_in_dim(block_tile, offset, GROUP, 0)
        alive = offset + positions < live_count
        targets = jnp.where(alive, tile_ids, tile_count)
        contrib = jnp.einsum(
            "bsc,bsr->bcr", blocks_now, weighted[sound_ids], preferred_element_type=jnp.float32
        )
        return running + jax.ops.segment_sum(contrib, targets, num_segments=tile_count)

    start_sum = jnp.zeros((tile_count, footprints.shape[2], width), jnp.float32)
    return lax.fori_loop(0, rounds, turn, start_sum)


def per_device(
    footprints, block_sounding, block_tile, block_count, observations, obs_weight, prior_std
):
    live_count = block_count[0]
    share_rows = prior_std.shape[1]
    tile_count = share_rows * lax.axis_size("orbit")
    sb_count = observations.shape[0]
    weight = obs_weight[:, :, None]
    prior_scale = prior_std[0][:, :, None]

    def reduce_tiles(partial_value):
        return lax.psum_scatter(partial_value, "orbit", scatter_dimension=0, tiled=True)

    def inner_sum(first_vec, second_vec):
        return lax.psum(jnp.sum(first_vec * second_vec, axis=(0, 1)), ("orbit", "region"))

    def apply_transpose(weighted):
        return reduce_tiles(
            local_transpose(
                footprints, block_sounding, block_tile, live_count, weighted, tile_count
            )
        )

    weighted0 = (weight * observations).astype(jnp.bfloat16)
    right_side = prior_scale * apply_transpose(weighted0)
    iterate = jnp.zeros_like(right_side)
    residual = right_side
    direction = right_side
    norm_now = inner_sum(residual, residual)
    for iteration in range(ITERS):
        scaled = (prior_scale * direction).astype(jnp.bfloat16)
        partial_value = local_forward(
            footprints,
            block_sounding,
            block_tile,
            live_count,
            lax.all_gather(scaled, "orbit", axis=0, tiled=True),
            sb_count,
        )
        image = lax.psum(partial_value, "region")
        weighted = (weight * image).astype(jnp.bfloat16)
        product = direction + prior_scale * apply_transpose(weighted)
        step_size = norm_now / inner_sum(direction, product)
        iterate = iterate + step_size * direction
        residual = residual - step_size * product
        if iteration + 1 < ITERS:
            norm_next = inner_sum(residual, residual)
            direction = residual + norm_next / norm_now * direction
            norm_now = norm_next
    flux = prior_scale * iterate
    return (flux[None], residual[None])


def solution(mesh):
    return jax.shard_map(
        per_device,
        mesh=mesh,
        in_specs=(
            P(("orbit", "region"), None, None),
            P(("orbit", "region")),
            P(("orbit", "region")),
            P(("orbit", "region")),
            P("orbit", None, None),
            P("orbit", None),
            P("region", "orbit", None),
        ),
        out_specs=(P("region", "orbit", None, None), P("region", "orbit", None, None)),
        check_vma=False,
    )
```

profile of v0, /device:TPU:1, one launch (start us, length us, event | category | flops | bytes accessed | tf_op | source)
XLA Modules:
  0.0 1179.8 jit_solution(10084983206093327789)
XLA Ops:
  9.5 2.5 broadcast.40.clone.1
  11.9 106.8 %while.55 = (s32[]{:T(128)}, f32[32,256,128]{2,1,0:T(8,128)}, s32[]{:T(128)}, s32[]{:T(128)}, s32[320]{0:T(512)S(1)}, /*index=5*/bf16[320,64,256]{2,1,0:T(8,128)...) while((s32[]{:T(128)}, f32[32,256,128]{2,1,0:T(8,128)}, ...), condition=%wide.region_2.3_spmd.clone, body=%wide.region_0.2_spmd.clone.sunk | while | flops 270534016 | bytes 38803376 | solution.py:49
  13.4 6.1 fusion.47
  19.5 19.0 %scatter_fusion = f32[32,256,128]{2,1,0:T(8,128)} fusion(f32[32,256,128]{2,1,0:T(8,128)} %get-tuple-element.721, s32[64]{0:T(128)S(1)} %get-tuple-element.666, f32[64,256,128]{2,1,0:T(8,128)} %fusion.47), kind=kCustom, calls=%fused_computation.5.clone.clone.1 | custom fusion | flops 2097152 | bytes 25166080 | tf_op jit(solution)/shard_map/while/body/scatter-add | solution.py:46
  40.1 6.1 fusion.47
  46.2 18.9 %scatter_fusion = f32[32,256,128]{2,1,0:T(8,128)} fusion(f32[32,256,128]{2,1,0:T(8,128)} %get-tuple-element.721, s32[64]{0:T(128)S(1)} %get-tuple-element.666, f32[64,256,128]{2,1,0:T(8,128)} %fusion.47), kind=kCustom, calls=%fused_computation.5.clone.clone.1 | custom fusion | flops 2097152 | bytes 25166080 | tf_op jit(solution)/shard_map/while/body/scatter-add | solution.py:46
  66.6 6.1 fusion.47
  72.7 19.0 %scatter_fusion = f32[32,256,128]{2,1,0:T(8,128)} fusion(f32[32,256,128]{2,1,0:T(8,128)} %get-tuple-element.721, s32[64]{0:T(128)S(1)} %get-tuple-element.666, f32[64,256,128]{2,1,0:T(8,128)} %fusion.47), kind=kCustom, calls=%fused_computation.5.clone.clone.1 | custom fusion | flops 2097152 | bytes 25166080 | tf_op jit(solution)/shard_map/while/body/scatter-add | solution.py:46
  93.2 6.1 fusion.47
  99.3 19.4 %scatter_fusion = f32[32,256,128]{2,1,0:T(8,128)} fusion(f32[32,256,128]{2,1,0:T(8,128)} %get-tuple-element.721, s32[64]{0:T(128)S(1)} %get-tuple-element.666, f32[64,256,128]{2,1,0:T(8,128)} %fusion.47), kind=kCustom, calls=%fused_computation.5.clone.clone.1 | custom fusion | flops 2097152 | bytes 25166080 | tf_op jit(solution)/shard_map/while/body/scatter-add | solution.py:46
  118.8 109.6 %reduce-scatter.4.cloned.1.call-done = f32[1,256,128]{2,1,0:T(8,128)} async-done(((f32[32,256,128]{2,1,0:T(8,128)}), f32[1,256,128]{2,1,0:T(8,128)}) %reduce-scatter.4.cloned.1.call-update) | async-done | bytes 131088 | tf_op jit(solution)/shard_map/reduce_scatter | solution.py:63
  230.2 46.2 %all-gather.3.cloned.1.call-done = bf16[32,256,128]{2,1,0:T(8,128)(2,1)} async-done(((bf16[1,256,128]{2,1,0:T(8,128)(2,1)}), bf16[32,256,128]{2,1,0:T(8,128)(2,1)}) %all-gather.3.cloned.1.call-update) | async-done | bytes 2097168 | tf_op jit(solution)/shard_map/all_gather | solution.py:88
  276.5 51.1 %while.56 = (s32[]{:T(128)}, f32[32,64,128]{2,1,0:T(8,128)S(1)}, s32[]{:T(128)}, s32[]{:T(128)}, s32[320]{0:T(512)S(1)}, /*index=5*/bf16[320,64,256]{2,1,0:T(8,1...) while((s32[]{:T(128)}, f32[32,64,128]{2,1,0:T(8,128)S(1)}, ...), condition=%wide.region_8.9_spmd.clone, body=%wide.region_6.8_spmd.clone.sunk | while | flops 268961152 | bytes 23074740 | solution.py:28
  277.3 4.6 gather_fusion.1
  281.9 3.7 fusion.50
  285.6 3.7 scatter_fusion.1
  290.1 4.6 gather_fusion.1
  294.7 3.7 fusion.50
  298.3 3.7 scatter_fusion.1
  302.8 4.6 gather_fusion.1
  307.4 3.7 fusion.50
  311.1 3.7 scatter_fusion.1
  315.6 4.6 gather_fusion.1
  320.2 3.7 fusion.50
  323.9 3.7 scatter_fusion.1
  328.7 55.4 %all-reduce.4.cloned.1.call-done = f32[32,64,128]{2,1,0:T(8,128)} async-done(((f32[32,64,128]{2,1,0:T(8,128)}), f32[32,64,128]{2,1,0:T(8,128)}) %all-reduce.4.cloned.1.call-update) | async-done | bytes 1048592 | tf_op jit(solution)/shard_map/psum | solution.py:91
  388.2 106.8 %while.57 = (s32[]{:T(128)}, f32[32,256,128]{2,1,0:T(8,128)}, s32[]{:T(128)}, s32[]{:T(128)}, s32[320]{0:T(512)S(1)}, /*index=5*/bf16[320,64,256]{2,1,0:T(8,128)...) while((s32[]{:T(128)}, f32[32,256,128]{2,1,0:T(8,128)}, ...), condition=%wide.region_12.13_spmd.clone, body=%wide.region_10.12_spmd.clone.sunk | while | flops 270534016 | bytes 38803376 | solution.py:49
  389.6 6.1 fusion.53
  395.8 19.0 %scatter_fusion.2 = f32[32,256,128]{2,1,0:T(8,128)} fusion(f32[32,256,128]{2,1,0:T(8,128)} %get-tuple-element.793, s32[64]{0:T(128)S(1)} %get-tuple-element.686, f32[64,256,128]{2,1,0:T(8,128)} %fusion.53), kind=kCustom, calls=%fused_computation.7.clone.clone.1 | custom fusion | flops 2097152 | bytes 25166080 | tf_op jit(solution)/shard_map/while/body/scatter-add | solution.py:46
  416.3 6.1 fusion.53
  422.4 18.9 %scatter_fusion.2 = f32[32,256,128]{2,1,0:T(8,128)} fusion(f32[32,256,128]{2,1,0:T(8,128)} %get-tuple-element.793, s32[64]{0:T(128)S(1)} %get-tuple-element.686, f32[64,256,128]{2,1,0:T(8,128)} %fusion.53), kind=kCustom, calls=%fused_computation.7.clone.clone.1 | custom fusion | flops 2097152 | bytes 25166080 | tf_op jit(solution)/shard_map/while/body/scatter-add | solution.py:46
  442.8 6.1 fusion.53
  448.9 19.0 %scatter_fusion.2 = f32[32,256,128]{2,1,0:T(8,128)} fusion(f32[32,256,128]{2,1,0:T(8,128)} %get-tuple-element.793, s32[64]{0:T(128)S(1)} %get-tuple-element.686, f32[64,256,128]{2,1,0:T(8,128)} %fusion.53), kind=kCustom, calls=%fused_computation.7.clone.clone.1 | custom fusion | flops 2097152 | bytes 25166080 | tf_op jit(solution)/shard_map/while/body/scatter-add | solution.py:46
  469.4 6.1 fusion.53
  475.5 19.4 %scatter_fusion.2 = f32[32,256,128]{2,1,0:T(8,128)} fusion(f32[32,256,128]{2,1,0:T(8,128)} %get-tuple-element.793, s32[64]{0:T(128)S(1)} %get-tuple-element.686, f32[64,256,128]{2,1,0:T(8,128)} %fusion.53), kind=kCustom, calls=%fused_computation.7.clone.clone.1 | custom fusion | flops 2097152 | bytes 25166080 | tf_op jit(solution)/shard_map/while/body/scatter-add | solution.py:46
  495.0 108.4 %reduce-scatter.6.cloned.1.call-done = f32[1,256,128]{2,1,0:T(8,128)} async-done(((f32[32,256,128]{2,1,0:T(8,128)}), f32[1,256,128]{2,1,0:T(8,128)}) %reduce-scatter.6.cloned.1.call-update) | async-done | bytes 131088 | tf_op jit(solution)/shard_map/reduce_scatter | solution.py:63
  604.4 65.9 %all-reduce = (f32[128]{0:T(128)S(1)}, f32[128]{0:T(128)S(1)}) all-reduce(f32[128]{0:T(128)S(1)} %get-tuple-element.343, f32[128]{0:T(128)S(1)} %get-tuple-element.342), channel_id=1, replica_groups=mesh['orbit'=32,'region'=4] {'orbit','region'}, use_global_device_ids=true, to_apply=%region_5.6 | all-reduce | flops 256 | bytes 2048 | tf_op jit(solution)/shard_map/psum | solution.py:66
  671.4 62.7 %psum.45 = f32[128]{0:T(128)S(1)} all-reduce(f32[128]{0:T(128)S(1)} %multiply_reduce_fusion.1), channel_id=1, replica_groups=mesh['orbit'=32,'region'=4] {'orbit','region'}, use_global_device_ids=true, to_apply=%region_17.18 | all-reduce | flops 128 | bytes 1024 | tf_op jit(solution)/shard_map/psum | solution.py:66
  735.8 41.3 %all-gather.5.cloned.1.call-done = bf16[32,256,128]{2,1,0:T(8,128)(2,1)} async-done(((bf16[1,256,128]{2,1,0:T(8,128)(2,1)}), bf16[32,256,128]{2,1,0:T(8,128)(2,1)}) %all-gather.5.cloned.1.call-update) | async-done | bytes 2097168 | tf_op jit(solution)/shard_map/all_gather | solution.py:88
  777.2 51.1 %while.58 = (s32[]{:T(128)}, f32[32,64,128]{2,1,0:T(8,128)S(1)}, s32[]{:T(128)}, s32[]{:T(128)}, s32[320]{0:T(512)S(1)}, /*index=5*/bf16[320,64,256]{2,1,0:T(8,1...) while((s32[]{:T(128)}, f32[32,64,128]{2,1,0:T(8,128)S(1)}, ...), condition=%wide.region_20.21_spmd.clone, body=%wide.region_18.20_spmd.clone.sunk | while | flops 268961152 | bytes 23074740 | solution.py:28
  778.0 4.6 gather_fusion.3
  782.6 3.7 fusion.56
  786.3 3.7 scatter_fusion.3
  790.7 4.6 gather_fusion.3
  795.3 3.7 fusion.56
  799.0 3.7 scatter_fusion.3
  803.5 4.6 gather_fusion.3
  808.1 3.7 fusion.56
  811.8 3.7 scatter_fusion.3
  816.3 4.6 gather_fusion.3
  820.9 3.7 fusion.56
  824.6 3.7 scatter_fusion.3
  829.4 55.4 %all-reduce.6.cloned.1.call-done = f32[32,64,128]{2,1,0:T(8,128)} async-done(((f32[32,64,128]{2,1,0:T(8,128)}), f32[32,64,128]{2,1,0:T(8,128)}) %all-reduce.6.cloned.1.call-update) | async-done | bytes 1048592 | tf_op jit(solution)/shard_map/psum | solution.py:91
  888.9 106.8 %while.59 = (s32[]{:T(128)}, f32[32,256,128]{2,1,0:T(8,128)}, s32[]{:T(128)}, s32[]{:T(128)}, s32[320]{0:T(512)S(1)}, /*index=5*/bf16[320,64,256]{2,1,0:T(8,128)...) while((s32[]{:T(128)}, f32[32,256,128]{2,1,0:T(8,128)}, ...), condition=%wide.region_24.25_spmd.clone, body=%wide.region_22.24_spmd.clone.sunk | while | flops 270534016 | bytes 38803376 | solution.py:49
  890.4 6.1 fusion.59
  896.5 19.0 %scatter_fusion.4 = f32[32,256,128]{2,1,0:T(8,128)} fusion(f32[32,256,128]{2,1,0:T(8,128)} %get-tuple-element.865, s32[64]{0:T(128)S(1)} %get-tuple-element.706, f32[64,256,128]{2,1,0:T(8,128)} %fusion.59), kind=kCustom, calls=%fused_computation.9.clone.clone.1 | custom fusion | flops 2097152 | bytes 25166080 | tf_op jit(solution)/shard_map/while/body/scatter-add | solution.py:46
  917.0 6.1 fusion.59
  923.1 18.9 %scatter_fusion.4 = f32[32,256,128]{2,1,0:T(8,128)} fusion(f32[32,256,128]{2,1,0:T(8,128)} %get-tuple-element.865, s32[64]{0:T(128)S(1)} %get-tuple-element.706, f32[64,256,128]{2,1,0:T(8,128)} %fusion.59), kind=kCustom, calls=%fused_computation.9.clone.clone.1 | custom fusion | flops 2097152 | bytes 25166080 | tf_op jit(solution)/shard_map/while/body/scatter-add | solution.py:46
  943.5 6.1 fusion.59
  949.6 19.0 %scatter_fusion.4 = f32[32,256,128]{2,1,0:T(8,128)} fusion(f32[32,256,128]{2,1,0:T(8,128)} %get-tuple-element.865, s32[64]{0:T(128)S(1)} %get-tuple-element.706, f32[64,256,128]{2,1,0:T(8,128)} %fusion.59), kind=kCustom, calls=%fused_computation.9.clone.clone.1 | custom fusion | flops 2097152 | bytes 25166080 | tf_op jit(solution)/shard_map/while/body/scatter-add | solution.py:46
  970.1 6.1 fusion.59
  976.3 19.4 %scatter_fusion.4 = f32[32,256,128]{2,1,0:T(8,128)} fusion(f32[32,256,128]{2,1,0:T(8,128)} %get-tuple-element.865, s32[64]{0:T(128)S(1)} %get-tuple-element.706, f32[64,256,128]{2,1,0:T(8,128)} %fusion.59), kind=kCustom, calls=%fused_computation.9.clone.clone.1 | custom fusion | flops 2097152 | bytes 25166080 | tf_op jit(solution)/shard_map/while/body/scatter-add | solution.py:46
  995.7 108.5 %reduce-scatter.8.cloned.1.call-done = f32[1,256,128]{2,1,0:T(8,128)} async-done(((f32[32,256,128]{2,1,0:T(8,128)}), f32[1,256,128]{2,1,0:T(8,128)}) %reduce-scatter.8.cloned.1.call-update) | async-done | bytes 131088 | tf_op jit(solution)/shard_map/reduce_scatter | solution.py:63
  1105.3 65.9 %psum.47 = f32[128]{0:T(128)S(1)} all-reduce(f32[128]{0:T(128)S(1)} %multiply_reduce_fusion), channel_id=1, replica_groups=mesh['orbit'=32,'region'=4] {'orbit','region'}, use_global_device_ids=true, to_apply=%region_27.28 | all-reduce | flops 128 | bytes 1024 | tf_op jit(solution)/shard_map/psum | solution.py:66
  (98 shorter events, 44.0 us)
Async XLA Ops:
  7.2 4.8 copy-start.6
  7.2 4.8 copy-start.5
  7.2 221.3 %reduce-scatter.4.cloned.1.call-start = ((), (), s32[]{:S(2)}) async-start(), calls=%async_computation.3 | async-start | bytes 4325376 | tf_op jit(solution)/shard_map/reduce_scatter | solution.py:63
  118.7 109.7 %copy-start.7 = (f32[1,1,256]{2,1,0:T(1,128)S(1)}, f32[1,1,256]{2,1,0:T(1,128)}, u32[]{:S(2)}) copy-start(f32[1,1,256]{2,1,0:T(1,128)} %param.23) | copy-start | bytes 3076
  118.7 157.7 %all-gather.3.cloned.1.call-start = ((), (), s32[]{:S(2)}) async-start(), calls=%async_computation.4 | async-start | bytes 2162688 | tf_op jit(solution)/shard_map/all_gather | solution.py:88
  230.1 154.0 %all-reduce.4.cloned.1.call-start = ((), (), s32[]{:S(2)}) async-start(), calls=%async_computation.5 | async-start | bytes 2097152 | tf_op jit(solution)/shard_map/psum | solution.py:91
  276.5 107.6 %copy-start.4 = (f32[32,64]{1,0:T(8,128)S(1)}, f32[32,64]{1,0:T(8,128)}, u32[]{:S(2)}) copy-start(f32[32,64]{1,0:T(8,128)} %param.22) | copy-start | bytes 24580
  327.6 1.0 copy-start
  328.7 274.7 %reduce-scatter.6.cloned.1.call-start = ((), (), s32[]{:S(2)}) async-start(), calls=%async_computation.6 | async-start | bytes 4325376 | tf_op jit(solution)/shard_map/reduce_scatter | solution.py:63
  495.0 108.5 %copy-start.2 = (f32[1,256,128]{2,1,0:T(8,128)S(1)}, f32[1,256,128]{2,1,0:T(8,128)}, u32[]{:S(2)}) copy-start(f32[1,256,128]{2,1,0:T(8,128)} %reduce-scatter.4.cloned.1.call-done) | copy-start | bytes 393220
  495.0 282.1 %all-gather.5.cloned.1.call-start = ((), (), s32[]{:S(2)}) async-start(), calls=%async_computation.7 | async-start | bytes 2162688 | tf_op jit(solution)/shard_map/all_gather | solution.py:88
  735.7 149.1 %all-reduce.6.cloned.1.call-start = ((), (), s32[]{:S(2)}) async-start(), calls=%async_computation.8 | async-start | bytes 2097152 | tf_op jit(solution)/shard_map/psum | solution.py:91
  828.3 1.0 copy-start.1
  829.4 274.9 %reduce-scatter.8.cloned.1.call-start = ((), (), s32[]{:S(2)}) async-start(), calls=%async_computation.9 | async-start | bytes 4325376 | tf_op jit(solution)/shard_map/reduce_scatter | solution.py:63
  995.7 108.6 %copy-start.3 = (f32[1,256,128]{2,1,0:T(8,128)S(1)}, f32[1,256,128]{2,1,0:T(8,128)}, u32[]{:S(2)}) copy-start(f32[1,256,128]{2,1,0:T(8,128)} %reduce-scatter.6.cloned.1.call-done) | copy-start | bytes 393220
Sparse Core Ops, SparseCore 0:
  118.9 109.5 reduce-scatter.3
  231.3 45.0 all-gather.2
  328.8 55.2 all-reduce.3
  495.1 108.2 reduce-scatter.5
  735.8 41.2 all-gather.4
  829.5 55.3 all-reduce.5
  995.8 108.3 reduce-scatter.7
where the time goes:
time: 1180 us
  waiting for transfers between devices  525 us (44%)
  other arithmetic  286 us (24%)
  blocking collectives  194 us (16%)
  matrix products  103 us (9%)
  local copies, waits for them, and re-layouts  55.5 us (5%)
  between operations  14.9 us (1%)
    reduce_scatter x3, waiting for transfers between devices, reduce_tiles(): lax.psum_scatter(partial_value, 'orbit', scatter_dimension=0, tiled=True)  327 us
    scatter-add x12, other arithmetic, turn(): jax.ops.segment_sum(contrib, targets, num_segments=tile_count)  229 us
    psum x3, blocking collectives, inner_sum(): lax.psum(jnp.sum(first_vec * second_vec, axis=(0, 1)), ('orbit', 'region'))  194 us
    psum x2, waiting for transfers between devices, per_device(): image = lax.psum(partial_value, 'region')  111 us
    all_gather x2, waiting for transfers between devices, per_device(): lax.all_gather(scaled, 'orbit', axis=0, tiled=True)  87.6 us
    dot_general x12, matrix products, turn(): jnp.einsum('bsc,bsr->bcr', blocks_now, weighted[sound_ids], preferred_ele...  73.4 us
    gather x8, local copies, waits for them, and re-layouts, turn(): whole[tile_ids]  36.8 us
    scatter-add x8, other arithmetic, turn(): jax.ops.segment_sum(products, targets, num_segments=sb_count)  29.7 us
  transfers between devices with their start and end apart: 7, of which 7 were waited for; matrix products, arithmetic and copies ran while one was open for 0% of the time, Pallas kernels for 0%

commit v1 on v0

--- a/solution.py
+++ b/solution.py
@@ -5,6 +5,10 @@
 
 ITERS = 2
 GROUP = 64
+
+
+def remake_pools(load, peer_axis, shard_axis):
+    return lax.psum(lax.psum(load, axis_name=peer_axis), axis_name=shard_axis)
 
 
 def local_forward(footprints, block_sounding, block_tile, live_count, whole, sb_count):
@@ -63,7 +67,7 @@
         return lax.psum_scatter(partial_value, "orbit", scatter_dimension=0, tiled=True)
 
     def inner_sum(first_vec, second_vec):
-        return lax.psum(jnp.sum(first_vec * second_vec, axis=(0, 1)), ("orbit", "region"))
+        return remake_pools(jnp.sum(first_vec * second_vec, axis=(0, 1)), "orbit", "region")
 
     def apply_transpose(weighted):
         return reduce_tiles(

time: 1180 us -> 1210 us (1.025)
  blocking collectives: 194 us -> 217 us
    psum x3 -> x6, blocking collectives: 194 us -> 217 us  [remake_pools(): return lax.psum(lax.psum(load, axis_name=peer_axis), axis_name=shard_axis)]
where the time goes in v1:
time: 1210 us; the launch traced here: 1200 us
  waiting for transfers between devices  525 us (43%)
  other arithmetic  286 us (24%)
  blocking collectives  217 us (18%)
  matrix products  103 us (9%)
  local copies, waits for them, and re-layouts  55.5 us (5%)
  between operations  14.9 us (1%)
    reduce_scatter x3, waiting for transfers between devices, reduce_tiles(): lax.psum_scatter(partial_value, 'orbit', scatter_dimension=0, tiled=True)  327 us
    scatter-add x12, other arithmetic, turn(): jax.ops.segment_sum(contrib, targets, num_segments=tile_count)  229 us
    psum x6, blocking collectives, remake_pools(): return lax.psum(lax.psum(load, axis_name=peer_axis), axis_name=shard_axis)  217 us
    psum x2, waiting for transfers between devices, per_device(): image = lax.psum(partial_value, 'region')  111 us
    all_gather x2, waiting for transfers between devices, per_device(): lax.all_gather(scaled, 'orbit', axis=0, tiled=True)  87.5 us
    dot_general x12, matrix products, turn(): jnp.einsum('bsc,bsr->bcr', blocks_now, weighted[sound_ids], preferred_ele...  73.4 us
    gather x8, local copies, waits for them, and re-layouts, turn(): whole[tile_ids]  36.8 us
    scatter-add x8, other arithmetic, turn(): jax.ops.segment_sum(products, targets, num_segments=sb_count)  29.7 us
  transfers between devices with their start and end apart: 7, of which 7 were waited for; matrix products, arithmetic and copies ran while one was open for 0% of the time, Pallas kernels for 0%

profile of v1, /device:TPU:1, one launch (start us, length us, event | category | flops | bytes accessed | tf_op | source)
XLA Modules:
  0.0 1202.0 jit_solution(5460878508863329491)
XLA Ops:
  11.9 106.8 %while.55 = (s32[]{:T(128)}, f32[32,256,128]{2,1,0:T(8,128)}, s32[]{:T(128)}, s32[]{:T(128)}, s32[320]{0:T(512)S(1)}, /*index=5*/bf16[320,64,256]{2,1,0:T(8,128)...) while((s32[]{:T(128)}, f32[32,256,128]{2,1,0:T(8,128)}, ...), condition=%wide.region_2.3_spmd.clone, body=%wide.region_0.2_spmd.clone.sunk | while | flops 270534016 | bytes 38803376 | solution.py:53
  13.4 6.1 fusion.47
  19.5 19.0 %scatter_fusion = f32[32,256,128]{2,1,0:T(8,128)} fusion(f32[32,256,128]{2,1,0:T(8,128)} %get-tuple-element.723, s32[64]{0:T(128)S(1)} %get-tuple-element.668, f32[64,256,128]{2,1,0:T(8,128)} %fusion.47), kind=kCustom, calls=%fused_computation.5.clone.clone.1 | custom fusion | flops 2097152 | bytes 25166080 | tf_op jit(solution)/shard_map/while/body/scatter-add | solution.py:50
  40.1 6.1 fusion.47
  46.2 18.9 %scatter_fusion = f32[32,256,128]{2,1,0:T(8,128)} fusion(f32[32,256,128]{2,1,0:T(8,128)} %get-tuple-element.723, s32[64]{0:T(128)S(1)} %get-tuple-element.668, f32[64,256,128]{2,1,0:T(8,128)} %fusion.47), kind=kCustom, calls=%fused_computation.5.clone.clone.1 | custom fusion | flops 2097152 | bytes 25166080 | tf_op jit(solution)/shard_map/while/body/scatter-add | solution.py:50
  66.6 6.1 fusion.47
  72.7 19.0 %scatter_fusion = f32[32,256,128]{2,1,0:T(8,128)} fusion(f32[32,256,128]{2,1,0:T(8,128)} %get-tuple-element.723, s32[64]{0:T(128)S(1)} %get-tuple-element.668, f32[64,256,128]{2,1,0:T(8,128)} %fusion.47), kind=kCustom, calls=%fused_computation.5.clone.clone.1 | custom fusion | flops 2097152 | bytes 25166080 | tf_op jit(solution)/shard_map/while/body/scatter-add | solution.py:50
  93.2 6.1 fusion.47
  99.3 19.4 %scatter_fusion = f32[32,256,128]{2,1,0:T(8,128)} fusion(f32[32,256,128]{2,1,0:T(8,128)} %get-tuple-element.723, s32[64]{0:T(128)S(1)} %get-tuple-element.668, f32[64,256,128]{2,1,0:T(8,128)} %fusion.47), kind=kCustom, calls=%fused_computation.5.clone.clone.1 | custom fusion | flops 2097152 | bytes 25166080 | tf_op jit(solution)/shard_map/while/body/scatter-add | solution.py:50
  118.8 109.6 %reduce-scatter.4.cloned.1.call-done = f32[1,256,128]{2,1,0:T(8,128)} async-done(((f32[32,256,128]{2,1,0:T(8,128)}), f32[1,256,128]{2,1,0:T(8,128)}) %reduce-scatter.4.cloned.1.call-update) | async-done | bytes 131088 | tf_op jit(solution)/shard_map/reduce_scatter | solution.py:67
  230.2 46.2 %all-gather.3.cloned.1.call-done = bf16[32,256,128]{2,1,0:T(8,128)(2,1)} async-done(((bf16[1,256,128]{2,1,0:T(8,128)(2,1)}), bf16[32,256,128]{2,1,0:T(8,128)(2,1)}) %all-gather.3.cloned.1.call-update) | async-done | bytes 2097168 | tf_op jit(solution)/shard_map/all_gather | solution.py:92
  276.5 51.1 %while.56 = (s32[]{:T(128)}, f32[32,64,128]{2,1,0:T(8,128)S(1)}, s32[]{:T(128)}, s32[]{:T(128)}, s32[320]{0:T(512)S(1)}, /*index=5*/bf16[320,64,256]{2,1,0:T(8,1...) while((s32[]{:T(128)}, f32[32,64,128]{2,1,0:T(8,128)S(1)}, ...), condition=%wide.region_9.10_spmd.clone, body=%wide.region_7.9_spmd.clone.sunk | while | flops 268961152 | bytes 23074740 | solution.py:32
  277.3 4.6 gather_fusion.1
  281.9 3.7 fusion.50
  285.6 3.7 scatter_fusion.1
  290.1 4.6 gather_fusion.1
  294.7 3.7 fusion.50
  298.3 3.7 scatter_fusion.1
  302.8 4.6 gather_fusion.1
  307.4 3.7 fusion.50
  311.1 3.7 scatter_fusion.1
  315.6 4.6 gather_fusion.1
  323.9 3.7 scatter_fusion.1
  328.7 55.4 %all-reduce.5.cloned.1.call-done = f32[32,64,128]{2,1,0:T(8,128)} async-done(((f32[32,64,128]{2,1,0:T(8,128)}), f32[32,64,128]{2,1,0:T(8,128)}) %all-reduce.5.cloned.1.call-update) | async-done | bytes 1048592 | tf_op jit(solution)/shard_map/psum | solution.py:95
  388.2 106.8 %while.57 = (s32[]{:T(128)}, f32[32,256,128]{2,1,0:T(8,128)}, s32[]{:T(128)}, s32[]{:T(128)}, s32[320]{0:T(512)S(1)}, /*index=5*/bf16[320,64,256]{2,1,0:T(8,128)...) while((s32[]{:T(128)}, f32[32,256,128]{2,1,0:T(8,128)}, ...), condition=%wide.region_13.14_spmd.clone, body=%wide.region_11.13_spmd.clone.sunk | while | flops 270534016 | bytes 38803376 | solution.py:53
  389.6 6.1 fusion.53
  395.8 19.0 %scatter_fusion.2 = f32[32,256,128]{2,1,0:T(8,128)} fusion(f32[32,256,128]{2,1,0:T(8,128)} %get-tuple-element.795, s32[64]{0:T(128)S(1)} %get-tuple-element.688, f32[64,256,128]{2,1,0:T(8,128)} %fusion.53), kind=kCustom, calls=%fused_computation.7.clone.clone.1 | custom fusion | flops 2097152 | bytes 25166080 | tf_op jit(solution)/shard_map/while/body/scatter-add | solution.py:50
  416.3 6.1 fusion.53
  422.4 18.9 %scatter_fusion.2 = f32[32,256,128]{2,1,0:T(8,128)} fusion(f32[32,256,128]{2,1,0:T(8,128)} %get-tuple-element.795, s32[64]{0:T(128)S(1)} %get-tuple-element.688, f32[64,256,128]{2,1,0:T(8,128)} %fusion.53), kind=kCustom, calls=%fused_computation.7.clone.clone.1 | custom fusion | flops 2097152 | bytes 25166080 | tf_op jit(solution)/shard_map/while/body/scatter-add | solution.py:50
  442.8 6.1 fusion.53
  448.9 19.0 %scatter_fusion.2 = f32[32,256,128]{2,1,0:T(8,128)} fusion(f32[32,256,128]{2,1,0:T(8,128)} %get-tuple-element.795, s32[64]{0:T(128)S(1)} %get-tuple-element.688, f32[64,256,128]{2,1,0:T(8,128)} %fusion.53), kind=kCustom, calls=%fused_computation.7.clone.clone.1 | custom fusion | flops 2097152 | bytes 25166080 | tf_op jit(solution)/shard_map/while/body/scatter-add | solution.py:50
  469.4 6.1 fusion.53
  475.5 19.4 %scatter_fusion.2 = f32[32,256,128]{2,1,0:T(8,128)} fusion(f32[32,256,128]{2,1,0:T(8,128)} %get-tuple-element.795, s32[64]{0:T(128)S(1)} %get-tuple-element.688, f32[64,256,128]{2,1,0:T(8,128)} %fusion.53), kind=kCustom, calls=%fused_computation.7.clone.clone.1 | custom fusion | flops 2097152 | bytes 25166080 | tf_op jit(solution)/shard_map/while/body/scatter-add | solution.py:50
  495.0 108.4 %reduce-scatter.6.cloned.1.call-done = f32[1,256,128]{2,1,0:T(8,128)} async-done(((f32[32,256,128]{2,1,0:T(8,128)}), f32[1,256,128]{2,1,0:T(8,128)}) %reduce-scatter.6.cloned.1.call-update) | async-done | bytes 131088 | tf_op jit(solution)/shard_map/reduce_scatter | solution.py:67
  604.4 64.4 %all-reduce = (f32[128]{0:T(128)S(1)}, f32[128]{0:T(128)S(1)}) all-reduce(f32[128]{0:T(128)S(1)} %get-tuple-element.343, f32[128]{0:T(128)S(1)} %get-tuple-element.342), channel_id=1, replica_groups=mesh['orbit'=32,'region'=4] {'orbit'}, use_global_device_ids=true, to_apply=%region_5.6 | all-reduce | flops 256 | bytes 2048 | tf_op jit(solution)/shard_map/psum | solution.py:11
  668.8 8.4 all-reduce.1
  678.3 65.1 %psum.75 = f32[128]{0:T(128)S(1)} all-reduce(f32[128]{0:T(128)S(1)} %multiply_reduce_fusion.1), channel_id=1, replica_groups=mesh['orbit'=32,'region'=4] {'orbit'}, use_global_device_ids=true, to_apply=%region_19.20 | all-reduce | flops 128 | bytes 1024 | tf_op jit(solution)/shard_map/psum | solution.py:11
  743.3 6.0 psum.76
  751.1 41.2 %all-gather.5.cloned.1.call-done = bf16[32,256,128]{2,1,0:T(8,128)(2,1)} async-done(((bf16[1,256,128]{2,1,0:T(8,128)(2,1)}), bf16[32,256,128]{2,1,0:T(8,128)(2,1)}) %all-gather.5.cloned.1.call-update) | async-done | bytes 2097168 | tf_op jit(solution)/shard_map/all_gather | solution.py:92
  792.4 51.3 %while.58 = (s32[]{:T(128)}, f32[32,64,128]{2,1,0:T(8,128)S(1)}, s32[]{:T(128)}, s32[]{:T(128)}, s32[320]{0:T(512)S(1)}, /*index=5*/bf16[320,64,256]{2,1,0:T(8,1...) while((s32[]{:T(128)}, f32[32,64,128]{2,1,0:T(8,128)S(1)}, ...), condition=%wide.region_23.24_spmd.clone, body=%wide.region_21.23_spmd.clone.sunk | while | flops 268961152 | bytes 23074740 | solution.py:32
  793.3 4.6 gather_fusion.3
  797.9 3.7 fusion.56
  801.6 3.7 scatter_fusion.3
  806.1 4.6 gather_fusion.3
  810.7 3.7 fusion.56
  814.4 3.7 scatter_fusion.3
  818.9 4.6 gather_fusion.3
  823.5 3.7 fusion.56
  827.2 3.7 scatter_fusion.3
  831.6 4.6 gather_fusion.3
  839.9 3.7 scatter_fusion.3
  844.8 55.4 %all-reduce.7.cloned.1.call-done = f32[32,64,128]{2,1,0:T(8,128)} async-done(((f32[32,64,128]{2,1,0:T(8,128)}), f32[32,64,128]{2,1,0:T(8,128)}) %all-reduce.7.cloned.1.call-update) | async-done | bytes 1048592 | tf_op jit(solution)/shard_map/psum | solution.py:95
  904.2 106.8 %while.59 = (s32[]{:T(128)}, f32[32,256,128]{2,1,0:T(8,128)}, s32[]{:T(128)}, s32[]{:T(128)}, s32[320]{0:T(512)S(1)}, /*index=5*/bf16[320,64,256]{2,1,0:T(8,128)...) while((s32[]{:T(128)}, f32[32,256,128]{2,1,0:T(8,128)}, ...), condition=%wide.region_27.28_spmd.clone, body=%wide.region_25.27_spmd.clone.sunk | while | flops 270534016 | bytes 38803376 | solution.py:53
  905.7 6.1 fusion.59
  911.8 19.0 %scatter_fusion.4 = f32[32,256,128]{2,1,0:T(8,128)} fusion(f32[32,256,128]{2,1,0:T(8,128)} %get-tuple-element.867, s32[64]{0:T(128)S(1)} %get-tuple-element.708, f32[64,256,128]{2,1,0:T(8,128)} %fusion.59), kind=kCustom, calls=%fused_computation.9.clone.clone.1 | custom fusion | flops 2097152 | bytes 25166080 | tf_op jit(solution)/shard_map/while/body/scatter-add | solution.py:50
  932.3 6.1 fusion.59
  938.5 18.9 %scatter_fusion.4 = f32[32,256,128]{2,1,0:T(8,128)} fusion(f32[32,256,128]{2,1,0:T(8,128)} %get-tuple-element.867, s32[64]{0:T(128)S(1)} %get-tuple-element.708, f32[64,256,128]{2,1,0:T(8,128)} %fusion.59), kind=kCustom, calls=%fused_computation.9.clone.clone.1 | custom fusion | flops 2097152 | bytes 25166080 | tf_op jit(solution)/shard_map/while/body/scatter-add | solution.py:50
  958.8 6.1 fusion.59
  965.0 19.0 %scatter_fusion.4 = f32[32,256,128]{2,1,0:T(8,128)} fusion(f32[32,256,128]{2,1,0:T(8,128)} %get-tuple-element.867, s32[64]{0:T(128)S(1)} %get-tuple-element.708, f32[64,256,128]{2,1,0:T(8,128)} %fusion.59), kind=kCustom, calls=%fused_computation.9.clone.clone.1 | custom fusion | flops 2097152 | bytes 25166080 | tf_op jit(solution)/shard_map/while/body/scatter-add | solution.py:50
  985.5 6.1 fusion.59
  991.6 19.4 %scatter_fusion.4 = f32[32,256,128]{2,1,0:T(8,128)} fusion(f32[32,256,128]{2,1,0:T(8,128)} %get-tuple-element.867, s32[64]{0:T(128)S(1)} %get-tuple-element.708, f32[64,256,128]{2,1,0:T(8,128)} %fusion.59), kind=kCustom, calls=%fused_computation.9.clone.clone.1 | custom fusion | flops 2097152 | bytes 25166080 | tf_op jit(solution)/shard_map/while/body/scatter-add | solution.py:50
  1011.0 108.5 %reduce-scatter.8.cloned.1.call-done = f32[1,256,128]{2,1,0:T(8,128)} async-done(((f32[32,256,128]{2,1,0:T(8,128)}), f32[1,256,128]{2,1,0:T(8,128)}) %reduce-scatter.8.cloned.1.call-update) | async-done | bytes 131088 | tf_op jit(solution)/shard_map/reduce_scatter | solution.py:67
  1120.6 64.3 %psum.78 = f32[128]{0:T(128)S(1)} all-reduce(f32[128]{0:T(128)S(1)} %multiply_reduce_fusion), channel_id=1, replica_groups=mesh['orbit'=32,'region'=4] {'orbit'}, use_global_device_ids=true, to_apply=%region_30.31 | all-reduce | flops 128 | bytes 1024 | tf_op jit(solution)/shard_map/psum | solution.py:11
  1185.0 8.4 psum.79
  (101 shorter events, 53.8 us)
Async XLA Ops:
  7.2 4.8 copy-start.6
  7.2 4.8 copy-start.5
  7.2 221.3 %reduce-scatter.4.cloned.1.call-start = ((), (), s32[]{:S(2)}) async-start(), calls=%async_computation.3 | async-start | bytes 4325376 | tf_op jit(solution)/shard_map/reduce_scatter | solution.py:67
  118.7 109.7 %copy-start.7 = (f32[1,1,256]{2,1,0:T(1,128)S(1)}, f32[1,1,256]{2,1,0:T(1,128)}, u32[]{:S(2)}) copy-start(f32[1,1,256]{2,1,0:T(1,128)} %param.23) | copy-start | bytes 3076
  118.7 157.7 %all-gather.3.cloned.1.call-start = ((), (), s32[]{:S(2)}) async-start(), calls=%async_computation.4 | async-start | bytes 2162688 | tf_op jit(solution)/shard_map/all_gather | solution.py:92
  230.1 154.0 %all-reduce.5.cloned.1.call-start = ((), (), s32[]{:S(2)}) async-start(), calls=%async_computation.5 | async-start | bytes 2097152 | tf_op jit(solution)/shard_map/psum | solution.py:95
  276.5 107.6 %copy-start.4 = (f32[32,64]{1,0:T(8,128)S(1)}, f32[32,64]{1,0:T(8,128)}, u32[]{:S(2)}) copy-start(f32[32,64]{1,0:T(8,128)} %param.22) | copy-start | bytes 24580
  327.6 1.0 copy-start
  328.7 274.7 %reduce-scatter.6.cloned.1.call-start = ((), (), s32[]{:S(2)}) async-start(), calls=%async_computation.6 | async-start | bytes 4325376 | tf_op jit(solution)/shard_map/reduce_scatter | solution.py:67
  495.0 108.5 %copy-start.2 = (f32[1,256,128]{2,1,0:T(8,128)S(1)}, f32[1,256,128]{2,1,0:T(8,128)}, u32[]{:S(2)}) copy-start(f32[1,256,128]{2,1,0:T(8,128)} %reduce-scatter.4.cloned.1.call-done) | copy-start | bytes 393220
  495.0 297.3 %all-gather.5.cloned.1.call-start = ((), (), s32[]{:S(2)}) async-start(), calls=%async_computation.7 | async-start | bytes 2162688 | tf_op jit(solution)/shard_map/all_gather | solution.py:92
  751.0 149.2 %all-reduce.7.cloned.1.call-start = ((), (), s32[]{:S(2)}) async-start(), calls=%async_computation.8 | async-start | bytes 2097152 | tf_op jit(solution)/shard_map/psum | solution.py:95
  843.7 1.0 copy-start.1
  844.7 274.8 %reduce-scatter.8.cloned.1.call-start = ((), (), s32[]{:S(2)}) async-start(), calls=%async_computation.9 | async-start | bytes 4325376 | tf_op jit(solution)/shard_map/reduce_scatter | solution.py:67
  1011.0 108.6 %copy-start.3 = (f32[1,256,128]{2,1,0:T(8,128)S(1)}, f32[1,256,128]{2,1,0:T(8,128)}, u32[]{:S(2)}) copy-start(f32[1,256,128]{2,1,0:T(8,128)} %reduce-scatter.6.cloned.1.call-done) | copy-start | bytes 393220
Sparse Core Ops, SparseCore 0:
  118.9 109.5 reduce-scatter.3
  231.3 45.0 all-gather.2
  328.8 55.2 all-reduce.4
  495.1 108.2 reduce-scatter.5
  751.1 41.1 all-gather.4
  844.8 55.2 all-reduce.6
  1011.1 108.3 reduce-scatter.7
